TPU v7x, 128 devices: a whole 4x4x4 slice. The times are simulated.
128 devices in a mesh: section: 4 (over z), seq: 32 (over y, x, core).
Axes of the slice: x: 4, y: 4, z: 4, core: 2. Of those that a mesh axis runs over, the one named last changes fastest.
Arguments:
- queries: bfloat16 [4, 4096, 8192], P('section', 'seq'), may hold values from -24 to 24
- keys: bfloat16 [4, 4096, 1024], P('section', 'seq'), may hold values from -24 to 24
- values: bfloat16 [4, 4096, 1024], P('section', 'seq'), may hold values from -6 to 6
- block_mask: int32 [4, 32, 32], P('section'), may hold values from 0 to 1, as said below
- block_live: int32 [4, 32], P('section'), may hold values from 1 to 128, as said below
Outputs:
- passed_context: bfloat16 [4, 4096, 8192], P('section', 'seq')
Inputs may be any that keep to these rules, and one draw needn't show every extreme that they name: block_mask[m, i, j] is 1 exactly when block j is block i or one of its ancestors in micro-batch m's tree: the first 16 blocks form a chain, each later block hangs below the chain's last block or a later block of lower index. `block_live`: the first 16 blocks of every micro-batch are full, its last block holds one live token.
All inputs are finite; a program needn't handle non-finite values.
Results may differ from a plain program's by a relative error of at most 0.0049.
Values may be sent and summed in bfloat16 or wider, within the bound.
A program may use at most 128 MiB of HBM per device.

v0:
```python
import jax
import jax.numpy as jnp
from jax import lax
from jax.sharding import PartitionSpec as P

QUERY_HEADS = 64
KEY_VALUE_HEADS = 8
HEAD_SIZE = 128


def side_by_side(arrays, axis, dim, along):
    both = jnp.concatenate(arrays, axis=along)
    result, at, done = (lax.all_gather(both, axis, axis=dim, tiled=True), 0, [])
    for a in arrays:
        done.append(lax.slice_in_dim(result, at, at + a.shape[along], axis=along))
        at += a.shape[along]
    return tuple(done)


def shifted(value, axis, by):
    count = lax.axis_size(axis)
    return lax.ppermute(value, axis, [(i, (i + by) % count) for i in range(count)])


def attend(qrows, qpos, keys_h, values_h, block_mask, block_live):
    total = keys_h.shape[0]
    nblk = block_mask.shape[0]
    width = total // nblk
    kpos = jnp.arange(total, dtype=jnp.int32)
    kblock = kpos // width
    key_live = kpos % width < jnp.repeat(block_live, width)
    qblock = qpos // width
    pick = (qblock[:, None] == jnp.arange(nblk, dtype=jnp.int32)[None, :]).astype(jnp.float32)
    allowed = jnp.repeat(jnp.dot(pick, block_mask.astype(jnp.float32)) > 0.5, width, axis=1)
    allowed = (
        allowed
        & key_live[None, :]
        & ((kblock[None, :] != qblock[:, None]) | (kpos[None, :] <= qpos[:, None]))
    )
    q_live = (qpos % width).astype(jnp.float32) < jnp.dot(pick, block_live.astype(jnp.float32))
    scale = qrows.shape[-1] ** (-0.5)
    scores = jnp.einsum("rgd,kd->grk", qrows, keys_h, preferred_element_type=jnp.float32) * scale
    scores = jnp.where(allowed[None], scores, -1e30)
    top = jnp.max(scores, axis=-1, keepdims=True)
    expo = jnp.where(allowed[None], jnp.exp(scores - top), 0.0)
    weights = (expo / jnp.sum(expo, axis=-1, keepdims=True)).astype(jnp.bfloat16)
    context = jnp.einsum("grk,kd->rgd", weights, values_h, preferred_element_type=jnp.float32)
    return jnp.where(q_live[:, None, None], context, 0.0).astype(jnp.bfloat16)


def per_device(queries, keys, values, block_mask, block_live):
    masks = block_mask[0]
    live = block_live[0]
    token_rows = queries.shape[1]
    nseq = lax.axis_size("seq")
    gathered_full = token_rows * nseq
    query_group_size = QUERY_HEADS // KEY_VALUE_HEADS
    gathered_keys, gathered_values = side_by_side((keys, values), "seq", 1, 0)
    query_head_rows = (
        queries[0]
        .reshape(token_rows, KEY_VALUE_HEADS, query_group_size, HEAD_SIZE)
        .transpose(1, 0, 2, 3)
    )
    key_head_rows = (
        gathered_keys[0].reshape(gathered_full, KEY_VALUE_HEADS, HEAD_SIZE).transpose(1, 0, 2)
    )
    value_head_rows = (
        gathered_values[0].reshape(gathered_full, KEY_VALUE_HEADS, HEAD_SIZE).transpose(1, 0, 2)
    )
    qpos = lax.axis_index("seq") * token_rows + jnp.arange(token_rows, dtype=jnp.int32)

    def head_fn(items):
        return attend(items[0], qpos, items[1], items[2], masks, live)

    out = lax.map(head_fn, (query_head_rows, key_head_rows, value_head_rows))
    local = out.transpose(1, 0, 2, 3).reshape(1, token_rows, QUERY_HEADS * HEAD_SIZE)
    return shifted(local, "section", 1)


def solution(mesh):
    placed = (
        P("section", "seq", None),
        P("section", "seq", None),
        P("section", "seq", None),
        P("section", None, None),
        P("section", None),
    )
    return jax.shard_map(
        per_device, mesh=mesh, in_specs=placed, out_specs=P("section", "seq", None), check_vma=False
    )
```

profile of v0, /device:TPU:31, one launch (start us, length us, event | category | flops | bytes accessed | tf_op | source)
XLA Modules:
  0.0 333.4 jit_solution(1779972675151198218)
XLA Ops:
  9.7 3.2 copy.12
  14.5 76.0 %all-gather.2.cloned.1.call-done = bf16[2,4096,1024]{1,2,0:T(8,128)(2,1)} async-done(((bf16[2,128,1024]{1,2,0:T(8,128)(2,1)}), bf16[2,4096,1024]{1,2,0:T(8,128)(2,1)}) %all-gather.2.cloned.1.call-update) | async-done | bytes 16777232 | tf_op jit(solution)/shard_map/all_gather | solution.py:13
  90.6 11.7 %fusion.74 = (bf16[1,4096,1024]{1,2,0:T(8,128)(2,1)}, bf16[1,4096,1024]{1,2,0:T(8,128)(2,1)}) fusion(bf16[2,4096,1024]{1,2,0:T(8,128)(2,1)} %all-gather.2.cloned.1.call-done), kind=kLoop, calls=%fused_computation.78 | loop fusion | bytes 33554432 | tf_op jit(solution)/shard_map/slice | solution.py:15
  102.2 171.9 %while.18 = (s32[]{:T(128)}, bf16[8,128,8,128]{1,3,2,0:T(8,128)(2,1)}, f32[128]{0:T(128)S(1)}, bf16[8,4096,128]{1,2,0:T(8,128)(2,1)}, bf16[32,32]{1,0:T(8,128)(2...) while((s32[]{:T(128)}, ...), condition=%wide.region_3.4_spmd.clone.clone, body=%wide.region_0.3_spmd.clone.clone.sunk | while | flops 2180067328 | bytes 37813740 | solution.py:75
  104.0 11.7 %fusion.93 = (f32[8,128]{1,0:T(8,128)S(1)}, f32[8,128,4096]{1,2,0:T(8,128)}) fusion(pred[128,4096]{0,1:T(8,128)(4,1)S(1)} %fusion.92, bf16[8,4096,128]{1,2,0:T(8,128)(2,1)} %get-tuple-element.473, s32[]{:T(128)} %get-tuple-element.457, bf16[8,128,8,128]{1,3,2,0:T(8,128)(2,1)S(1)} %get-tuple-element.474), kind=kOutput, calls=%fused_computation.77.clone.1 | convolution fusion | flops 1094717440 | bytes 19141632 | tf_op jit(solution)/shard_map/while/body/eval_jaxpr/sub | solution.py:45
  115.6 8.1 %fusion.95 = bf16[8,128,8,128]{1,3,2,0:T(8,128)(2,1)} fusion(bf16[8,128,8,128]{1,3,2,0:T(8,128)(2,1)} %get-tuple-element.458, s32[]{:T(128)} %get-tuple-element.457, f32[8,128,4096]{1,2,0:T(8,128)} %get-tuple-element.445, f32[8,128]{1,0:T(8,128)S(1)} %get-tuple-element.446, bf16[8,4096,128]{1,2,0:T(8,128)(2,1)} %get-tuple-element.470, ...), kind=kOutput, calls=%fused_computation.20.clone.1 | convolution fusion | flops 1082392576 | bytes 18093184 | tf_op jit(solution)/shard_map/while/body/eval_jaxpr/grk,kd->rgd/dot_general | solution.py:47
  125.4 11.7 %fusion.93 = (f32[8,128]{1,0:T(8,128)S(1)}, f32[8,128,4096]{1,2,0:T(8,128)}) fusion(pred[128,4096]{0,1:T(8,128)(4,1)S(1)} %fusion.92, bf16[8,4096,128]{1,2,0:T(8,128)(2,1)} %get-tuple-element.473, s32[]{:T(128)} %get-tuple-element.457, bf16[8,128,8,128]{1,3,2,0:T(8,128)(2,1)S(1)} %get-tuple-element.474), kind=kOutput, calls=%fused_computation.77.clone.1 | convolution fusion | flops 1094717440 | bytes 19141632 | tf_op jit(solution)/shard_map/while/body/eval_jaxpr/sub | solution.py:45
  137.1 8.1 %fusion.95 = bf16[8,128,8,128]{1,3,2,0:T(8,128)(2,1)} fusion(bf16[8,128,8,128]{1,3,2,0:T(8,128)(2,1)} %get-tuple-element.458, s32[]{:T(128)} %get-tuple-element.457, f32[8,128,4096]{1,2,0:T(8,128)} %get-tuple-element.445, f32[8,128]{1,0:T(8,128)S(1)} %get-tuple-element.446, bf16[8,4096,128]{1,2,0:T(8,128)(2,1)} %get-tuple-element.470, ...), kind=kOutput, calls=%fused_computation.20.clone.1 | convolution fusion | flops 1082392576 | bytes 18093184 | tf_op jit(solution)/shard_map/while/body/eval_jaxpr/grk,kd->rgd/dot_general | solution.py:47
  145.5 1.4 fusion.92
  146.9 11.7 %fusion.93 = (f32[8,128]{1,0:T(8,128)S(1)}, f32[8,128,4096]{1,2,0:T(8,128)}) fusion(pred[128,4096]{0,1:T(8,128)(4,1)S(1)} %fusion.92, bf16[8,4096,128]{1,2,0:T(8,128)(2,1)} %get-tuple-element.473, s32[]{:T(128)} %get-tuple-element.457, bf16[8,128,8,128]{1,3,2,0:T(8,128)(2,1)S(1)} %get-tuple-element.474), kind=kOutput, calls=%fused_computation.77.clone.1 | convolution fusion | flops 1094717440 | bytes 19141632 | tf_op jit(solution)/shard_map/while/body/eval_jaxpr/sub | solution.py:45
  158.6 8.1 %fusion.95 = bf16[8,128,8,128]{1,3,2,0:T(8,128)(2,1)} fusion(bf16[8,128,8,128]{1,3,2,0:T(8,128)(2,1)} %get-tuple-element.458, s32[]{:T(128)} %get-tuple-element.457, f32[8,128,4096]{1,2,0:T(8,128)} %get-tuple-element.445, f32[8,128]{1,0:T(8,128)S(1)} %get-tuple-element.446, bf16[8,4096,128]{1,2,0:T(8,128)(2,1)} %get-tuple-element.470, ...), kind=kOutput, calls=%fused_computation.20.clone.1 | convolution fusion | flops 1082392576 | bytes 18093184 | tf_op jit(solution)/shard_map/while/body/eval_jaxpr/grk,kd->rgd/dot_general | solution.py:47
  167.0 1.4 fusion.92
  168.4 11.7 %fusion.93 = (f32[8,128]{1,0:T(8,128)S(1)}, f32[8,128,4096]{1,2,0:T(8,128)}) fusion(pred[128,4096]{0,1:T(8,128)(4,1)S(1)} %fusion.92, bf16[8,4096,128]{1,2,0:T(8,128)(2,1)} %get-tuple-element.473, s32[]{:T(128)} %get-tuple-element.457, bf16[8,128,8,128]{1,3,2,0:T(8,128)(2,1)S(1)} %get-tuple-element.474), kind=kOutput, calls=%fused_computation.77.clone.1 | convolution fusion | flops 1094717440 | bytes 19141632 | tf_op jit(solution)/shard_map/while/body/eval_jaxpr/sub | solution.py:45
  180.1 8.1 %fusion.95 = bf16[8,128,8,128]{1,3,2,0:T(8,128)(2,1)} fusion(bf16[8,128,8,128]{1,3,2,0:T(8,128)(2,1)} %get-tuple-element.458, s32[]{:T(128)} %get-tuple-element.457, f32[8,128,4096]{1,2,0:T(8,128)} %get-tuple-element.445, f32[8,128]{1,0:T(8,128)S(1)} %get-tuple-element.446, bf16[8,4096,128]{1,2,0:T(8,128)(2,1)} %get-tuple-element.470, ...), kind=kOutput, calls=%fused_computation.20.clone.1 | convolution fusion | flops 1082392576 | bytes 18093184 | tf_op jit(solution)/shard_map/while/body/eval_jaxpr/grk,kd->rgd/dot_general | solution.py:47
  189.9 11.7 %fusion.93 = (f32[8,128]{1,0:T(8,128)S(1)}, f32[8,128,4096]{1,2,0:T(8,128)}) fusion(pred[128,4096]{0,1:T(8,128)(4,1)S(1)} %fusion.92, bf16[8,4096,128]{1,2,0:T(8,128)(2,1)} %get-tuple-element.473, s32[]{:T(128)} %get-tuple-element.457, bf16[8,128,8,128]{1,3,2,0:T(8,128)(2,1)S(1)} %get-tuple-element.474), kind=kOutput, calls=%fused_computation.77.clone.1 | convolution fusion | flops 1094717440 | bytes 19141632 | tf_op jit(solution)/shard_map/while/body/eval_jaxpr/sub | solution.py:45
  201.6 8.1 %fusion.95 = bf16[8,128,8,128]{1,3,2,0:T(8,128)(2,1)} fusion(bf16[8,128,8,128]{1,3,2,0:T(8,128)(2,1)} %get-tuple-element.458, s32[]{:T(128)} %get-tuple-element.457, f32[8,128,4096]{1,2,0:T(8,128)} %get-tuple-element.445, f32[8,128]{1,0:T(8,128)S(1)} %get-tuple-element.446, bf16[8,4096,128]{1,2,0:T(8,128)(2,1)} %get-tuple-element.470, ...), kind=kOutput, calls=%fused_computation.20.clone.1 | convolution fusion | flops 1082392576 | bytes 18093184 | tf_op jit(solution)/shard_map/while/body/eval_jaxpr/grk,kd->rgd/dot_general | solution.py:47
  211.4 11.7 %fusion.93 = (f32[8,128]{1,0:T(8,128)S(1)}, f32[8,128,4096]{1,2,0:T(8,128)}) fusion(pred[128,4096]{0,1:T(8,128)(4,1)S(1)} %fusion.92, bf16[8,4096,128]{1,2,0:T(8,128)(2,1)} %get-tuple-element.473, s32[]{:T(128)} %get-tuple-element.457, bf16[8,128,8,128]{1,3,2,0:T(8,128)(2,1)S(1)} %get-tuple-element.474), kind=kOutput, calls=%fused_computation.77.clone.1 | convolution fusion | flops 1094717440 | bytes 19141632 | tf_op jit(solution)/shard_map/while/body/eval_jaxpr/sub | solution.py:45
  223.1 8.1 %fusion.95 = bf16[8,128,8,128]{1,3,2,0:T(8,128)(2,1)} fusion(bf16[8,128,8,128]{1,3,2,0:T(8,128)(2,1)} %get-tuple-element.458, s32[]{:T(128)} %get-tuple-element.457, f32[8,128,4096]{1,2,0:T(8,128)} %get-tuple-element.445, f32[8,128]{1,0:T(8,128)S(1)} %get-tuple-element.446, bf16[8,4096,128]{1,2,0:T(8,128)(2,1)} %get-tuple-element.470, ...), kind=kOutput, calls=%fused_computation.20.clone.1 | convolution fusion | flops 1082392576 | bytes 18093184 | tf_op jit(solution)/shard_map/while/body/eval_jaxpr/grk,kd->rgd/dot_general | solution.py:47
  232.9 11.7 %fusion.93 = (f32[8,128]{1,0:T(8,128)S(1)}, f32[8,128,4096]{1,2,0:T(8,128)}) fusion(pred[128,4096]{0,1:T(8,128)(4,1)S(1)} %fusion.92, bf16[8,4096,128]{1,2,0:T(8,128)(2,1)} %get-tuple-element.473, s32[]{:T(128)} %get-tuple-element.457, bf16[8,128,8,128]{1,3,2,0:T(8,128)(2,1)S(1)} %get-tuple-element.474), kind=kOutput, calls=%fused_computation.77.clone.1 | convolution fusion | flops 1094717440 | bytes 19141632 | tf_op jit(solution)/shard_map/while/body/eval_jaxpr/sub | solution.py:45
  244.6 8.1 %fusion.95 = bf16[8,128,8,128]{1,3,2,0:T(8,128)(2,1)} fusion(bf16[8,128,8,128]{1,3,2,0:T(8,128)(2,1)} %get-tuple-element.458, s32[]{:T(128)} %get-tuple-element.457, f32[8,128,4096]{1,2,0:T(8,128)} %get-tuple-element.445, f32[8,128]{1,0:T(8,128)S(1)} %get-tuple-element.446, bf16[8,4096,128]{1,2,0:T(8,128)(2,1)} %get-tuple-element.470, ...), kind=kOutput, calls=%fused_computation.20.clone.1 | convolution fusion | flops 1082392576 | bytes 18093184 | tf_op jit(solution)/shard_map/while/body/eval_jaxpr/grk,kd->rgd/dot_general | solution.py:47
  254.4 11.7 %fusion.93 = (f32[8,128]{1,0:T(8,128)S(1)}, f32[8,128,4096]{1,2,0:T(8,128)}) fusion(pred[128,4096]{0,1:T(8,128)(4,1)S(1)} %fusion.92, bf16[8,4096,128]{1,2,0:T(8,128)(2,1)} %get-tuple-element.473, s32[]{:T(128)} %get-tuple-element.457, bf16[8,128,8,128]{1,3,2,0:T(8,128)(2,1)S(1)} %get-tuple-element.474), kind=kOutput, calls=%fused_computation.77.clone.1 | convolution fusion | flops 1094717440 | bytes 19141632 | tf_op jit(solution)/shard_map/while/body/eval_jaxpr/sub | solution.py:45
  266.1 8.1 %fusion.95 = bf16[8,128,8,128]{1,3,2,0:T(8,128)(2,1)} fusion(bf16[8,128,8,128]{1,3,2,0:T(8,128)(2,1)} %get-tuple-element.458, s32[]{:T(128)} %get-tuple-element.457, f32[8,128,4096]{1,2,0:T(8,128)} %get-tuple-element.445, f32[8,128]{1,0:T(8,128)S(1)} %get-tuple-element.446, bf16[8,4096,128]{1,2,0:T(8,128)(2,1)} %get-tuple-element.470, ...), kind=kOutput, calls=%fused_computation.20.clone.1 | convolution fusion | flops 1082392576 | bytes 18093184 | tf_op jit(solution)/shard_map/while/body/eval_jaxpr/grk,kd->rgd/dot_general | solution.py:47
  274.1 2.9 copy.17
  278.4 46.9 %collective-permute-done = bf16[1,128,8192]{2,1,0:T(8,128)(2,1)S(1)} collective-permute-done((bf16[1,128,8192]{2,1,0:T(8,128)(2,1)S(1)}, bf16[1,128,8192]{2,1,0:T(8,128)(2,1)S(1)}, u32[]{:S(2)}, u32[]{:S(2)}) %collective-permute-start) | collective-permute-done | bytes 2097184 | tf_op jit(solution)/shard_map/ppermute | solution.py:22
  (59 shorter events, 18.4 us)
Async XLA Ops:
  6.5 84.0 %all-gather.2.cloned.1.call-start = ((), (), s32[]{:S(2)}) async-start(), calls=%async_computation | async-start | bytes 17301504 | tf_op jit(solution)/shard_map/all_gather | solution.py:13
  14.5 87.7 %copy-start = (s32[1,32]{1,0:T(1,128)S(1)}, s32[1,32]{1,0:T(1,128)}, u32[]{:S(2)}) copy-start(s32[1,32]{1,0:T(1,128)} %param.11) | copy-start | bytes 388
  277.1 48.2 %collective-permute-start = (bf16[1,128,8192]{2,1,0:T(8,128)(2,1)S(1)}, bf16[1,128,8192]{2,1,0:T(8,128)(2,1)S(1)}, u32[]{:S(2)}, u32[]{:S(2)}) collective-permute-start(bf16[1,128,8192]{2,1,0:T(8,128)(2,1)S(1)} %copy.17), channel_id=1, source_target_pairs={{0,32},{32,64},{64,96},{96,0},{1,33},{33,65},{65,97},{97,1},{2,34}... | collective-permute-start | bytes 6291464 | tf_op jit(solution)/shard_map/ppermute | solution.py:22
Sparse Core Ops, SparseCore 0:
  9.8 80.7 all-gather.1
where the time goes:
time: 337 us; the launch traced here: 333 us
  matrix products  161 us (48%)
  waiting for transfers between devices  123 us (36%)
  local copies, waits for them, and re-layouts  21.3 us (6%)
  other arithmetic  13.7 us (4%)
  between operations  13.4 us (4%)
    sub x8, matrix products, attend(): expo = jnp.where(allowed[None], jnp.exp(scores - top), 0.0)  93.2 us
    all_gather x1, waiting for transfers between devices, side_by_side(): result, at, done = (lax.all_gather(both, axis, axis=dim, tiled=True), 0, [])  76 us
    dot_general x8, matrix products, attend(): jnp.einsum('grk,kd->rgd', weights, values_h, preferred_element_type=jnp.f...  64.8 us
    ppermute x1, waiting for transfers between devices, shifted(): lax.ppermute(value, axis, [(i, (i + by) % count) for i in range(count)])  46.9 us
    slice x1, local copies, waits for them, and re-layouts, side_by_side(): done.append(lax.slice_in_dim(result, at, at + a.shape[along], axis=along))  11.7 us
    and x8, other arithmetic, attend(): allowed & key_live[None, :]  11.3 us
    unnamed x6, local copies, waits for them, and re-layouts  6.78 us
  transfers between devices with their start and end apart: 2, of which 2 were waited for; matrix products, arithmetic and copies ran while one was open for 1% of the time, Pallas kernels for 0%

commit v1 on v0

v1 whole, which is shorter than its diff:
```python
import jax
import jax.numpy as jnp
from jax import lax
from jax.experimental import pallas as pl
from jax.experimental.pallas import tpu as pltpu
from jax.sharding import PartitionSpec as P

QUERY_HEADS = 64
KEY_VALUE_HEADS = 8
HEAD_SIZE = 128
BLK = 128
NB = 32
PHASES = 4
UNIT = 2
UNITS = 8 // UNIT
ROWS = 2 * BLK * UNIT
CH = 512
COEF = 1.4426950408889634 * HEAD_SIZE ** (-0.5)
NEG = -1e30


def col(start, size):
    return pl.ds(pl.multiple_of(start, 128), size)


def kernel(
    mask_ref, live_ref, q_hbm, k_hbm, v_hbm, out_hbm,
    kbuf, vbuf, qbuf, obuf, sbuf, bias, mbuf, mcbuf, lbuf, acc,
    r1, r2, r3, rq, ro, s1, s2, s3, sq, so,
):
    z = lax.axis_index("section")
    s = lax.axis_index("seq")
    core = lax.rem(s, 2)
    chip = s // 2
    x = lax.rem(chip, 4)
    y = chip // 4

    def at(xx, yy, kk):
        return {"seq": (lax.rem(yy, 4) * 4 + lax.rem(xx, 4)) * 2 + kk}

    def across(dz, kk):
        return {"section": lax.rem(z + dz, 4), "seq": chip * 2 + kk}

    other = {"seq": chip * 2 + 1 - core}

    def remote(src, dst, send, recv, dev):
        return pltpu.make_async_remote_copy(
            src_ref=src, dst_ref=dst, send_sem=send, recv_sem=recv,
            device_id=dev, device_id_type=pl.DeviceIdType.MESH,
        )

    barrier = pltpu.get_barrier_semaphore()
    partners = [other]
    for d in (1, 2, 3):
        for kk in (0, 1):
            partners.append(at(x + d, y, kk))
            partners.append(at(x, y + d, kk))
    for d in (1, 3):
        for kk in (0, 1):
            partners.append(across(d, kk))
    for dev in partners:
        pl.semaphore_signal(barrier, inc=1, device_id=dev, device_id_type=pl.DeviceIdType.MESH)
    pl.semaphore_wait(barrier, len(partners))

    pairs = ((k_hbm, kbuf), (v_hbm, vbuf))

    def stage1(p):
        for n, (src_hbm, buf) in enumerate(pairs):
            dst = buf.at[y, x, pl.ds(core * BLK, BLK), col(p * 128, 128)]
            for g in (0, 1):
                src = src_hbm.at[0, :, col((4 * g + p) * 128, 128)]
                @pl.when(core == g)
                def _():
                    pltpu.make_async_copy(src, dst, r1.at[p, n]).start()
                @pl.when(core != g)
                def _():
                    remote(src, dst, s1.at[n, 0], r1.at[p, n], other).start()
                for d in (1, 3, 2):
                    dev = at(x + d, y, 0) if g == 0 else at(x, y + d, 1)
                    remote(src, dst, s1.at[n, 3 * g + d], r1.at[p, n], dev).start()

    def queries(p):
        dst = qbuf.at[core, :, col(p * 1024, 1024)]
        pltpu.make_async_copy(q_hbm.at[0, :, col(core * 4096 + p * 1024, 1024)], dst, rq.at[p]).start()
        remote(q_hbm.at[0, :, col((1 - core) * 4096 + p * 1024, 1024)], dst, sq, rq.at[p], other).start()

    def wait_on(ref, sem):
        pltpu.make_async_copy(ref, ref, sem).wait()

    def stage2(p):
        for n, (_, buf) in enumerate(pairs):
            wait_on(buf.at[0, :, :, col(p * 128, 128)], r1.at[p, n])
        for n, (_, buf) in enumerate(pairs):
            for side, d in ((0, 1), (1, 3)):
                @pl.when(core == 0)
                def _():
                    slab = buf.at[y, :, :, col(p * 128, 128)]
                    remote(slab, slab, s2.at[n, side], r2.at[p, n, side], at(x, y + d, 0)).start()
                @pl.when(core == 1)
                def _():
                    slab = buf.at[:, x, :, col(p * 128, 128)]
                    remote(slab, slab, s2.at[n, side], r2.at[p, n, side], at(x + d, y, 1)).start()

    def stage3(p):
        for n, (_, buf) in enumerate(pairs):
            for side, d in ((0, 1), (1, 3)):
                wait_on(buf.at[0, :, :, col(p * 128, 128)], r2.at[p, n, side])
        for n, (_, buf) in enumerate(pairs):
            for side, d in ((0, 1), (1, 3)):
                @pl.when(core == 0)
                def _():
                    half = buf.at[lax.rem(y + 4 - d, 4), pl.ds(2 * side, 2), :, col(p * 128, 128)]
                    remote(half, half, s3.at[n, side], r3.at[p, n, side], at(x, y + d, 0)).start()
                @pl.when(core == 1)
                def _():
                    half = buf.at[pl.ds(2 * side, 2), lax.rem(x + 4 - d, 4), :, col(p * 128, 128)]
                    remote(half, half, s3.at[n, side], r3.at[p, n, side], at(x + d, y, 1)).start()

    def arrived(p):
        for n, (_, buf) in enumerate(pairs):
            for side in (0, 1):
                wait_on(buf.at[0, pl.ds(0, 2), :, col(p * 128, 128)], r3.at[p, n, side])
        wait_on(qbuf.at[:, :, col(p * 1024, 1024)], rq.at[p])

    stage1(0)
    queries(0)

    rows = lax.broadcasted_iota(jnp.int32, (BLK, BLK), 0)
    cols = lax.broadcasted_iota(jnp.int32, (BLK, BLK), 1)

    def fill(b, carry):
        for i in (0, 1):
            row = 2 * chip + i
            upto = live_ref[0, b] * mask_ref[0, row, b]
            own = jnp.where(b == row, 0, BLK)
            ok = (cols < upto) & (cols <= rows + own)
            bias[pl.ds(i * BLK, BLK), col(b * BLK, BLK)] = jnp.where(ok, 0.0, NEG)
        return carry

    lax.fori_loop(0, NB, fill, 0)

    chunks = (chip + 2) // 2
    plain = jnp.minimum((chip + 0) // 2, 4)

    def q_unit(p, u):
        parts = []
        for h in range(UNIT):
            part = qbuf[:, :, col(p * 1024 + (u * UNIT + h) * 128, 128)]
            parts.append(part.reshape(2 * BLK, HEAD_SIZE))
        return jnp.concatenate(parts, axis=0)

    def keys_of(buf, p, j):
        return buf[j // 2, pl.ds(lax.rem(j, 2) * 2, 2), :, col(p * 128, 128)].reshape(CH, HEAD_SIZE)

    def score(p, u, j, masked):
        slot = lax.rem(u, 2)
        sc = lax.dot_general(
            q_unit(p, u), keys_of(kbuf, p, j), (((1,), (1,)), ((), ())),
            preferred_element_type=jnp.float32,
        )
        if masked:
            add = bias[:, col(j * CH, CH)]
            sc = sc + jnp.concatenate([add] * UNIT, axis=0)
        sbuf[slot, :, col(j * CH, CH)] = sc
        top = mbuf[...]
        for t in range(CH // 128):
            top = jnp.maximum(top, sc[:, t * 128:(t + 1) * 128])
        mbuf[...] = top

    def weigh(p, u, j):
        slot = lax.rem(u, 2)
        mc = mcbuf[...]
        total = lbuf[...]
        parts = []
        for t in range(CH // 128):
            e = jnp.exp2(sbuf[slot, :, col(j * CH + t * 128, 128)] * COEF - mc)
            total = total + e
            parts.append(e.astype(jnp.bfloat16))
        lbuf[...] = total
        acc[...] += jnp.dot(
            jnp.concatenate(parts, axis=1), keys_of(vbuf, p, j), preferred_element_type=jnp.float32
        )

    def settle():
        top = jnp.max(mbuf[...], axis=1, keepdims=True) * COEF
        mcbuf[...] = jnp.broadcast_to(top, (ROWS, 128))
        mbuf[...] = jnp.full((ROWS, 128), -3e38, jnp.float32)
        lbuf[...] = jnp.zeros((ROWS, 128), jnp.float32)
        acc[...] = jnp.zeros((ROWS, HEAD_SIZE), jnp.float32)

    def loop(low, high, body):
        def step(j, carry):
            body(j)
            return carry
        lax.fori_loop(low, high, step, 0)

    def finish(p, u):
        out = acc[...] / jnp.sum(lbuf[...], axis=1, keepdims=True)
        here = lax.broadcasted_iota(jnp.int32, (BLK, HEAD_SIZE), 0)
        for i in (0, 1):
            keep = here < live_ref[0, 2 * chip + i]
            for h in range(UNIT):
                part = out[(2 * h + i) * BLK:(2 * h + i + 1) * BLK]
                obuf[i, :, col(p * 1024 + (u * UNIT + h) * 128, 128)] = jnp.where(keep, part, 0.0).astype(jnp.bfloat16)

    def send(p, u):
        for i in (0, 1):
            at_col = p * 1024 + u * (UNIT * 128)
            remote(
                obuf.at[i, :, col(at_col, UNIT * 128)],
                out_hbm.at[0, :, col(core * 4096 + at_col, UNIT * 128)],
                so.at[i], ro, across(1, i),
            ).start()

    mbuf[...] = jnp.full((ROWS, 128), -3e38, jnp.float32)
    stage2(0)
    stage1(1)
    queries(1)
    stage3(0)

    def phase(p, carry):
        @pl.when(p < 3)
        def _():
            stage2(p + 1)
        @pl.when(p < 2)
        def _():
            stage1(p + 2)
            queries(p + 2)
        arrived(p)
        loop(0, plain, lambda j: score(p, 0, j, False))
        loop(plain, chunks, lambda j: score(p, 0, j, True))
        settle()

        def unit(u, carry):
            def both(masked):
                def body(j):
                    score(p, u, j, masked)
                    weigh(p, u - 1, j)
                return body
            loop(0, plain, both(False))
            loop(plain, chunks, both(True))
            finish(p, u - 1)
            send(p, u - 1)
            settle()
            @pl.when((u == 2) & (p < 3))
            def _():
                stage3(p + 1)
            return carry

        lax.fori_loop(1, UNITS, unit, 0)
        loop(0, chunks, lambda j: weigh(p, UNITS - 1, j))
        finish(p, UNITS - 1)
        send(p, UNITS - 1)
        return carry

    lax.fori_loop(0, PHASES, phase, 0)

    wait_on(out_hbm.at[0], ro)
    for i in (0, 1):
        wait_on(obuf.at[i], so.at[i])
    wait_on(qbuf.at[0], sq)
    for n, (_, buf) in enumerate(pairs):
        for dest in range(7):
            ref = buf.at[0, pl.ds(0, 2), :, pl.ds(0, 128)]
            if dest == 0:
                wait_on(ref, s1.at[n, 0])
            else:
                wait_on(ref, s1.at[n, dest])
        for side in (0, 1):
            wait_on(buf.at[:, :, :, pl.ds(0, 128)], s2.at[n, side])
            wait_on(buf.at[pl.ds(0, 2), :, :, pl.ds(0, 128)], s3.at[n, side])


def per_device(queries, keys, values, block_mask, block_live):
    dma = pltpu.SemaphoreType.DMA
    smem = pl.BlockSpec(memory_space=pltpu.SMEM)
    hbm = pl.BlockSpec(memory_space=pl.ANY)
    return pl.pallas_call(
        kernel,
        out_shape=jax.ShapeDtypeStruct(queries.shape, queries.dtype),
        in_specs=[smem, smem, hbm, hbm, hbm],
        out_specs=hbm,
        scratch_shapes=[
            pltpu.VMEM((4, 4, 2 * BLK, 512), jnp.bfloat16),
            pltpu.VMEM((4, 4, 2 * BLK, 512), jnp.bfloat16),
            pltpu.VMEM((2, BLK, 4096), jnp.bfloat16),
            pltpu.VMEM((2, BLK, 4096), jnp.bfloat16),
            pltpu.VMEM((2, ROWS, NB * BLK), jnp.float32),
            pltpu.VMEM((2 * BLK, NB * BLK), jnp.float32),
            pltpu.VMEM((ROWS, 128), jnp.float32),
            pltpu.VMEM((ROWS, 128), jnp.float32),
            pltpu.VMEM((ROWS, 128), jnp.float32),
            pltpu.VMEM((ROWS, HEAD_SIZE), jnp.float32),
            dma((4, 2)), dma((4, 2, 2)), dma((4, 2, 2)), dma((4,)), dma,
            dma((2, 7)), dma((2, 2)), dma((2, 2)), dma, dma((2,)),
        ],
        compiler_params=pltpu.CompilerParams(
            collective_id=0, has_side_effects=True, vmem_limit_bytes=60 * 1024 * 1024
        ),
    )(block_mask, block_live, queries, keys, values)


def solution(mesh):
    placed = (
        P("section", "seq", None),
        P("section", "seq", None),
        P("section", "seq", None),
        P("section", None, None),
        P("section", None),
    )
    return jax.shard_map(
        per_device, mesh=mesh, in_specs=placed, out_specs=P("section", "seq", None), check_vma=False
    )
```

time: 337 us -> 122 us (0.36)
  matrix products: 161 us -> 0 us
  waiting for transfers between devices: 123 us -> 0 us
  Pallas kernels: 0 us -> 118 us
  local copies, waits for them, and re-layouts: 21.3 us -> 3.1 us
  other arithmetic: 13.7 us -> 0 us
  between operations: 13.4 us -> 0.01 us
    pallas_call x0 -> x1, Pallas kernels: none -> 118 us  [per_device(): pl.pallas_call(kernel, out_shape=jax.ShapeDtypeStruct(queries.shape, quer...]
    sub x8 -> x0, matrix products: 93.2 us -> none  [attend(): expo = jnp.where(allowed[None], jnp.exp(scores - top), 0.0)]
    all_gather x1 -> x0, waiting for transfers between devices: 76 us -> none  [side_by_side(): result, at, done = (lax.all_gather(both, axis, axis=dim, tiled=True), 0, [])]
    dot_general x17 -> x0, matrix products: 67.3 us -> none  [the longest x8 64.8 us: attend(): jnp.einsum('grk,kd->rgd', weights, values_h, preferred_element_type=jnp.f...]
    ppermute x1 -> x0, waiting for transfers between devices: 46.9 us -> none  [shifted(): lax.ppermute(value, axis, [(i, (i + by) % count) for i in range(count)])]
    slice x1 -> x0, local copies, waits for them, and re-layouts: 11.7 us -> none  [side_by_side(): done.append(lax.slice_in_dim(result, at, at + a.shape[along], axis=along))]
    and x8 -> x0, other arithmetic: 11.3 us -> none  [attend(): allowed & key_live[None, :]]
    unnamed x6 -> x1, local copies, waits for them, and re-layouts: 6.78 us -> 3.1 us
  transfers between devices with their start and end apart: 2 -> 0, of which waited for: 2 -> 0; matrix products, arithmetic and copies ran while one was open for 1% -> 0% of each run, Pallas kernels for 0% -> 0%
where the time goes in v1:
time: 122 us
  Pallas kernels  118 us (97%)
  local copies, waits for them, and re-layouts  3.1 us (3%)
    pallas_call x1, Pallas kernels, per_device(): pl.pallas_call(kernel, out_shape=jax.ShapeDtypeStruct(queries.shape, quer...  118 us
    unnamed x1, local copies, waits for them, and re-layouts  3.1 us

profile of v1, /device:TPU:31, one launch (start us, length us, event | category | flops | bytes accessed | tf_op | source)
XLA Modules:
  0.0 121.6 jit_solution(7156224899428213331)
XLA Ops:
  0.0 118.5 %shard_map.55 = bf16[1,128,8192]{2,1,0:T(8,128)(2,1)} custom-call(s32[1,32,32]{2,1,0:T(8,128)} %mask_ref.1, s32[1,32]{1,0:T(1,128)} %live_ref.1, bf16[1,128,8192]{2,1,0:T(8,128)(2,1)} %q_hbm.1, bf16[1,128,1024]{2,1,0:T(8,128)(2,1)} %k_hbm.1, bf16[1,128,1024]{2,1,0:T(8,128)(2,1)} %v_hbm.1), custom_call_target="tpu_custom_call" | custom-call | tf_op jit(solution)/shard_map/pallas_call | solution.py:278
  118.5 3.1 %copy.7 = bf16[1,128,8192]{2,1,0:T(8,128)(2,1)} copy(bf16[1,128,8192]{2,1,0:T(8,128)(2,1)} %shard_map.55) | data formatting | bytes 4194304

commit v2 on v1

v2 whole, which is shorter than its diff:
```python
import jax
import jax.numpy as jnp
from jax import lax
from jax.experimental import pallas as pl
from jax.experimental.pallas import tpu as pltpu
from jax.sharding import PartitionSpec as P

QUERY_HEADS = 64
KEY_VALUE_HEADS = 8
HEAD_SIZE = 128
BLK = 128
NB = 32
UNIT = 2
UNITS = 8 // UNIT
ROWS = 2 * BLK * UNIT
CH = 1024
STEP = 512
COEF = 1.4426950408889634 * HEAD_SIZE ** (-0.5)
NEG = -1e30


def col(start, size):
    return pl.ds(pl.multiple_of(start, 128), size)


def kernel(
    mask_ref, live_ref, q_hbm, k_hbm, v_hbm, out_hbm,
    kbuf, vbuf, kshift, vshift, qbuf, obuf, sbuf0, sbuf1, bias, reach, keep, mbuf, mcbuf, qs0, qs1, acc,
    r1, r2, r3, rq, rkv, rre, ro, s1, s2, s3, sq, sq3, skv, sre, so, so3, so4,
):
    z = lax.axis_index("section")
    s = lax.axis_index("seq")
    core = lax.rem(s, 2)
    chip = s // 2
    x = lax.rem(chip, 4)
    y = chip // 4
    last_row = y // 3

    def at(xx, yy, kk):
        return {"seq": (lax.rem(yy, 4) * 4 + lax.rem(xx, 4)) * 2 + kk}

    def across(dz, kk):
        return {"section": lax.rem(z + dz, 4), "seq": chip * 2 + kk}

    other = {"seq": chip * 2 + 1 - core}

    def remote(src, dst, send, recv, dev):
        return pltpu.make_async_remote_copy(
            src_ref=src, dst_ref=dst, send_sem=send, recv_sem=recv,
            device_id=dev, device_id_type=pl.DeviceIdType.MESH,
        )

    barrier = pltpu.get_barrier_semaphore()
    partners = [other]
    for d in (1, 2, 3):
        for kk in (0, 1):
            partners.append(at(x + d, y, kk))
            partners.append(at(x, y + d, kk))
    for d in (1, 3):
        for kk in (0, 1):
            partners.append(across(d, kk))
            partners.append({"section": lax.rem(z + d, 4), **at(x, y + d, kk)})
    for dev in partners:
        pl.semaphore_signal(barrier, inc=1, device_id=dev, device_id_type=pl.DeviceIdType.MESH)
    pl.semaphore_wait(barrier, len(partners))

    pairs = ((k_hbm, kbuf), (v_hbm, vbuf))
    shifts = (kshift, vshift)

    def stage1(p):
        for n, (src_hbm, buf) in enumerate(pairs):
            dst = buf.at[y, x, pl.ds(core * BLK, BLK), pl.ds(p * 128, 128)]
            for g in (0, 1):
                if p < 3:
                    src = src_hbm.at[0, :, pl.ds((4 * g + p) * 128, 128)]
                else:
                    src = shifts[n].at[:, pl.ds(g * 128, 128)]
                @pl.when(core == g)
                def _():
                    pltpu.make_async_copy(src, dst, r1.at[p, n]).start()
                @pl.when(core != g)
                def _():
                    remote(src, dst, s1.at[n, 0], r1.at[p, n], other).start()
                for d in (1, 3, 2):
                    dev = at(x + d, y, 0) if g == 0 else at(x, y + d, 1)
                    remote(src, dst, s1.at[n, 3 * g + d], r1.at[p, n], dev).start()

    def queries(p):
        dst = qbuf.at[p, core]
        pltpu.make_async_copy(q_hbm.at[0, :, col(core * 4096 + p * 1024, 1024)], dst, rq.at[p]).start()
        remote(q_hbm.at[0, :, col((1 - core) * 4096 + p * 1024, 1024)], dst, sq, rq.at[p], other).start()

    def shift_keys():
        for n, (src_hbm, _) in enumerate(pairs):
            for g in (0, 1):
                remote(
                    src_hbm.at[0, :, pl.ds((4 * g + 3) * 128, 128)], shifts[n].at[:, pl.ds(g * 128, 128)],
                    skv.at[n], rkv.at[n], across(1, core),
                ).start()

    def ahead(kk):
        return {"section": lax.rem(z + 1, 4), "seq": (chip - 12 * last_row) * 2 + kk}

    def shift_queries():
        for g in (0, 1):
            remote(
                q_hbm.at[0, :, pl.ds(g * 4096 + 3 * 1024, 1024)], qbuf.at[3 + last_row, core],
                sq3, rq.at[3 + last_row], ahead(g),
            ).start()

    def wait_on(ref, sem):
        pltpu.make_async_copy(ref, ref, sem).wait()

    lower, upper = (0, 1), (1, 3)
    is_first, is_second = core == 0, core == 1

    def row_in(rows):
        hit = y == rows[0]
        for r in rows[1:]:
            hit = hit | (y == r)
        return hit

    def plan(p):
        if p < 3:
            return dict(whole=((0, 1, 2), (0,)), half=((), (1,)), on=((1, 2), (0, 3)))
        return dict(whole=((0, 1, 3), (1,)), half=((2,), (0, 2)), on=((1, 3), (1, 3)))

    def moved(rows, d):
        return tuple((r + d) % 4 for r in rows)

    def second_rows(p):
        return is_second if p < 3 else is_second & (y < 3)

    def stage2(p):
        lane = pl.ds(p * 128, 128)
        for n, (_, buf) in enumerate(pairs):
            wait_on(buf.at[0, :, :, lane], r1.at[p, n])
        for n, (_, buf) in enumerate(pairs):
            for side, d in (lower, upper):
                def go(src, dev):
                    remote(src, src, s2.at[p // 3, n, side], r2.at[p, n, side], dev).start()
                for rows, part in ((plan(p)["whole"][side], pl.ds(0, 4)), (plan(p)["half"][side], pl.ds(2 * side, 2))):
                    if rows:
                        @pl.when(is_first & row_in(rows))
                        def _():
                            go(buf.at[y, part, :, lane], at(x, y + d, 0))
                @pl.when(second_rows(p))
                def _():
                    go(buf.at[:, x, :, lane], at(x + d, y, 1))

    def stage3(p):
        lane = pl.ds(p * 128, 128)
        for n, (_, buf) in enumerate(pairs):
            for side, d in (lower, upper):
                for rows, size in ((plan(p)["whole"][side], 4), (plan(p)["half"][side], 2)):
                    if rows:
                        @pl.when(is_first & row_in(moved(rows, d)))
                        def _():
                            wait_on(buf.at[0, pl.ds(0, size), :, lane], r2.at[p, n, side])
                @pl.when(second_rows(p))
                def _():
                    wait_on(buf.at[0, :, :, lane], r2.at[p, n, side])
        for n, (_, buf) in enumerate(pairs):
            for side, d in (lower, upper):
                def go(src, dev):
                    remote(src, src, s3.at[p // 3, n, side], r3.at[p, n, side], dev).start()
                @pl.when(is_first & row_in(plan(p)["on"][side]))
                def _():
                    go(buf.at[lax.rem(y + 4 - d, 4), pl.ds(2 * side, 2), :, lane], at(x, y + d, 0))
                @pl.when(second_rows(p))
                def _():
                    go(buf.at[pl.ds(2 * side, 2), lax.rem(x + 4 - d, 4), :, lane], at(x + d, y, 1))

    def arrived(p):
        for n, (_, buf) in enumerate(pairs):
            for side, d in (lower, upper):
                @pl.when((is_first & row_in(moved(plan(p)["on"][side], d))) | second_rows(p))
                def _():
                    wait_on(buf.at[0, pl.ds(0, 2), :, pl.ds(0, 128)], r3.at[p, n, side])

    stage1(0)
    queries(0)
    stage1(1)

    lanes = lax.broadcasted_iota(jnp.int32, (8, BLK), 1)
    first = lax.broadcasted_iota(jnp.int32, (8, BLK), 0) == 0

    def reach_of(b, carry):
        upto = [live_ref[0, b] * mask_ref[0, 2 * chip + i, b] for i in (0, 1)]
        reach[0, :, col((b - 16) * BLK, BLK)] = jnp.where(lanes < jnp.where(first, upto[0], upto[1]), 0.0, NEG)
        return carry

    lax.fori_loop(16, NB, reach_of, 0)
    stage2(0)
    shift_keys()
    remote(reach.at[0], reach.at[1 + last_row], sre, rre.at[last_row], ahead(core)).start()
    shift_queries()

    rows = lax.broadcasted_iota(jnp.int32, (BLK, BLK), 0)
    cols = lax.broadcasted_iota(jnp.int32, (BLK, BLK), 1)

    def fill(src, base):
        def one(b, carry):
            for i in (0, 1):
                line = reach[src, pl.ds(i, 1), col(jnp.maximum(b - 16, 0) * BLK, BLK)]
                line = jnp.where(b >= 16, line, 0.0)
                ok = cols <= rows + (base + i - b) * BLK
                bias[pl.ds(i * BLK, BLK), col(b * BLK, BLK)] = jnp.where(ok, line, NEG)
            return carry

        lax.fori_loop(0, NB, one, 0)
        for i in (0, 1):
            b = base + i
            line = reach[src, pl.ds(i, 1), col(jnp.maximum(b - 16, 0) * BLK, BLK)]
            line = jnp.where(b >= 16, line, 0.0)
            keep[i] = jnp.broadcast_to(line, (BLK, BLK)).T

    fill(0, 2 * chip)

    sbufs = (sbuf0, sbuf1)
    qbufs = (qs0, qs1)
    ones = jnp.ones((CH, 128), jnp.bfloat16)

    def split_queries(t, u):
        for h in range(UNIT):
            part = qbuf[t, :, :, pl.ds((u * UNIT + h) * 128, 128)]
            part = part.reshape(2 * BLK, HEAD_SIZE).astype(jnp.float32) * COEF
            high = part.astype(jnp.bfloat16)
            low = (part - high.astype(jnp.float32)).astype(jnp.bfloat16)
            here = pl.ds(h * 2 * BLK, 2 * BLK)
            qbufs[u % 2][here, pl.ds(0, 128)] = high
            qbufs[u % 2][here, pl.ds(128, 128)] = low

    def rows_of(buf, p, j):
        return buf[j, :, :, col(p * 128, 128)].reshape(CH, HEAD_SIZE)

    def score(p, u, j, masked):
        sbuf = sbufs[u % 2]
        k = rows_of(kbuf, p, j)
        top = mbuf[...]
        for t in range(CH // STEP):
            k_t = k[t * STEP:(t + 1) * STEP]
            sc = lax.dot_general(
                qbufs[u % 2][...], jnp.concatenate([k_t, k_t], axis=1), (((1,), (1,)), ((), ())),
                preferred_element_type=jnp.float32,
            )
            if masked:
                add = bias[:, col(j * CH + t * STEP, STEP)]
                sc = sc + jnp.concatenate([add] * UNIT, axis=0)
            sbuf[:, col(j * CH + t * STEP, STEP)] = sc
            for v in range(STEP // 128):
                top = jnp.maximum(top, sc[:, v * 128:(v + 1) * 128])
        mbuf[...] = top

    def weigh(p, u, j):
        sbuf = sbufs[u % 2]
        top = mcbuf[...]
        parts = []
        for t in range(CH // 128):
            e = jnp.exp2(sbuf[:, col(j * CH + t * 128, 128)] - top)
            parts.append(e.astype(jnp.bfloat16))
        acc[...] += jnp.dot(
            jnp.concatenate(parts, axis=1), jnp.concatenate([rows_of(vbuf, p, j), ones], axis=1),
            preferred_element_type=jnp.float32,
        )

    def settle():
        mcbuf[...] = jnp.broadcast_to(jnp.max(mbuf[...], axis=1, keepdims=True), (ROWS, 128))
        mbuf[...] = jnp.full((ROWS, 128), -3e38, jnp.float32)
        acc[...] = jnp.zeros((ROWS, 2 * HEAD_SIZE), jnp.float32)

    def loop(low, high, body):
        def step(j, carry):
            body(j)
            return carry
        lax.fori_loop(low, high, step, 0)

    def finish(t, u):
        out = acc[:, :HEAD_SIZE] / acc[:, HEAD_SIZE:]
        for i in (0, 1):
            alive = keep[i] > -1.0
            for h in range(UNIT):
                part = out[(2 * h + i) * BLK:(2 * h + i + 1) * BLK]
                obuf[t, i, :, pl.ds((u * UNIT + h) * 128, 128)] = jnp.where(alive, part, 0.0).astype(jnp.bfloat16)

    def send(t, u):
        width = UNIT * 128
        for i in (0, 1):
            src = obuf.at[t, i, :, pl.ds(u * width, width)]
            @pl.when(t < 3)
            def _():
                dst = out_hbm.at[0, :, col(core * 4096 + t * 1024 + u * width, width)]
                remote(src, dst, so.at[i], ro, across(1, i)).start()
            dst = out_hbm.at[0, :, col(core * 4096 + 3 * 1024 + u * width, width)]
            @pl.when((t == 3) & (core == i))
            def _():
                pltpu.make_async_copy(src, dst, ro).start()
            @pl.when((t == 3) & (core != i))
            def _():
                remote(src, dst, so3, ro, other).start()
            @pl.when(t == 4)
            def _():
                remote(src, dst, so4.at[i], ro, {"seq": (12 + x) * 2 + i}).start()

    mbuf[...] = jnp.full((ROWS, 128), -3e38, jnp.float32)
    stage3(0)
    stage2(1)
    stage1(2)
    queries(1)
    queries(2)
    for n in (0, 1):
        wait_on(shifts[n], rkv.at[n])
    stage1(3)

    def job(t, carry):
        p = jnp.minimum(t, 3)
        row = y + 3 * (t // 4)
        chunks = row + 1
        plain = jnp.minimum(row, 2)

        for part in range(4):
            @pl.when(t == part)
            def _():
                arrived(part)
        wait_on(qbuf.at[0], rq.at[t])
        @pl.when(t == 3)
        def _():
            wait_on(reach.at[1], rre.at[0])
            fill(1, 2 * chip)
        @pl.when(t == 4)
        def _():
            wait_on(reach.at[2], rre.at[1])
            fill(2, 2 * (12 + x))

        split_queries(t, 0)
        loop(0, plain, lambda j: score(p, 0, j, False))
        loop(plain, chunks, lambda j: score(p, 0, j, True))
        settle()

        for u in range(1, UNITS):
            split_queries(t, u)
            def both(masked):
                def body(j):
                    score(p, u, j, masked)
                    weigh(p, u - 1, j)
                return body
            loop(0, plain, both(False))
            loop(plain, chunks, both(True))
            finish(t, u - 1)
            send(t, u - 1)
            settle()
            if u == 1:
                @pl.when(t == 0)
                def _():
                    stage3(1)
                    stage2(2)
                    stage2(3)
                @pl.when(t == 1)
                def _():
                    stage3(2)
                    stage3(3)

        loop(0, chunks, lambda j: weigh(p, UNITS - 1, j))
        finish(t, UNITS - 1)
        send(t, UNITS - 1)
        return carry

    lax.fori_loop(0, 3 + (3 - y + 2) // 3 + (3 - y) // 3, job, 0)

    wait_on(out_hbm.at[0], ro)
    for i in (0, 1):
        wait_on(obuf.at[pl.ds(0, 3), i], so.at[i])
    @pl.when(y < 3)
    def _():
        wait_on(obuf.at[0, 0], so3)
    @pl.when(y == 0)
    def _():
        for i in (0, 1):
            wait_on(obuf.at[0, 0], so4.at[i])
    wait_on(qbuf.at[pl.ds(0, 3), 0], sq)
    wait_on(qbuf.at[0], sq3)
    wait_on(reach.at[0], sre)
    for n, (_, buf) in enumerate(pairs):
        wait_on(shifts[n], skv.at[n])
        for dest in range(7):
            wait_on(buf.at[0, pl.ds(0, 2), :, pl.ds(0, 128)], s1.at[n, dest])
        lane = pl.ds(0, 128)
        for g, p in ((0, 0), (1, 3)):
            times = pl.ds(0, 3) if g == 0 else pl.ds(0, 1)
            for side in (0, 1):
                for rows, size in ((plan(p)["whole"][side], 4), (plan(p)["half"][side], 2)):
                    if rows:
                        @pl.when(is_first & row_in(rows))
                        def _():
                            wait_on(buf.at[times, pl.ds(0, size), :, lane], s2.at[g, n, side])
                @pl.when(second_rows(p))
                def _():
                    wait_on(buf.at[times, pl.ds(0, 4), :, lane], s2.at[g, n, side])
                @pl.when((is_first & row_in(plan(p)["on"][side])) | second_rows(p))
                def _():
                    wait_on(buf.at[times, pl.ds(0, 2), :, lane], s3.at[g, n, side])


def per_device(queries, keys, values, block_mask, block_live):
    dma = pltpu.SemaphoreType.DMA
    smem = pl.BlockSpec(memory_space=pltpu.SMEM)
    hbm = pl.BlockSpec(memory_space=pl.ANY)
    return pl.pallas_call(
        kernel,
        out_shape=jax.ShapeDtypeStruct(queries.shape, queries.dtype),
        in_specs=[smem, smem, hbm, hbm, hbm],
        out_specs=hbm,
        scratch_shapes=[
            pltpu.VMEM((4, 4, 2 * BLK, 512), jnp.bfloat16),
            pltpu.VMEM((4, 4, 2 * BLK, 512), jnp.bfloat16),
            pltpu.VMEM((BLK, 256), jnp.bfloat16),
            pltpu.VMEM((BLK, 256), jnp.bfloat16),
            pltpu.VMEM((5, 2, BLK, 1024), jnp.bfloat16),
            pltpu.VMEM((5, 2, BLK, 1024), jnp.bfloat16),
            pltpu.VMEM((ROWS, NB * BLK), jnp.float32),
            pltpu.VMEM((ROWS, NB * BLK), jnp.float32),
            pltpu.VMEM((2 * BLK, NB * BLK), jnp.float32),
            pltpu.VMEM((3, 8, 16 * BLK), jnp.float32),
            pltpu.VMEM((2, BLK, BLK), jnp.float32),
            pltpu.VMEM((ROWS, 128), jnp.float32),
            pltpu.VMEM((ROWS, 128), jnp.float32),
            pltpu.VMEM((ROWS, 256), jnp.bfloat16),
            pltpu.VMEM((ROWS, 256), jnp.bfloat16),
            pltpu.VMEM((ROWS, 2 * HEAD_SIZE), jnp.float32),
            dma((4, 2)), dma((4, 2, 2)), dma((4, 2, 2)), dma((5,)), dma((2,)), dma((2,)), dma,
            dma((2, 7)), dma((2, 2, 2)), dma((2, 2, 2)), dma, dma, dma((2,)), dma, dma((2,)), dma, dma((2,)),
        ],
        compiler_params=pltpu.CompilerParams(
            collective_id=0, has_side_effects=True, vmem_limit_bytes=60 * 1024 * 1024
        ),
    )(block_mask, block_live, queries, keys, values)


def solution(mesh):
    placed = (
        P("section", "seq", None),
        P("section", "seq", None),
        P("section", "seq", None),
        P("section", None, None),
        P("section", None),
    )
    return jax.shard_map(
        per_device, mesh=mesh, in_specs=placed, out_specs=P("section", "seq", None), check_vma=False
    )
```

time: 122 us -> 90.1 us (0.74)
  Pallas kernels: 118 us -> 86.4 us
    pallas_call x1, Pallas kernels: 118 us -> 86.4 us  [per_device(): pl.pallas_call(kernel, out_shape=jax.ShapeDtypeStruct(queries.shape, quer...]
where the time goes in v2:
time: 90.1 us; the launch traced here: 89.5 us
  Pallas kernels  86.4 us (96%)
  local copies, waits for them, and re-layouts  3.1 us (3%)
    pallas_call x1, Pallas kernels, per_device(): pl.pallas_call(kernel, out_shape=jax.ShapeDtypeStruct(queries.shape, quer...  86.4 us
    unnamed x1, local copies, waits for them, and re-layouts  3.1 us

profile of v2, /device:TPU:31, one launch (start us, length us, event | category | flops | bytes accessed | tf_op | source)
XLA Modules:
  0.0 89.5 jit_solution(10090465496804775601)
XLA Ops:
  0.0 86.4 %shard_map.55 = bf16[1,128,8192]{2,1,0:T(8,128)(2,1)} custom-call(s32[1,32,32]{2,1,0:T(8,128)} %mask_ref.1, s32[1,32]{1,0:T(1,128)} %live_ref.1, bf16[1,128,8192]{2,1,0:T(8,128)(2,1)} %q_hbm.1, bf16[1,128,1024]{2,1,0:T(8,128)(2,1)} %k_hbm.1, bf16[1,128,1024]{2,1,0:T(8,128)(2,1)} %v_hbm.1), custom_call_target="tpu_custom_call" | custom-call | tf_op jit(solution)/shard_map/pallas_call | solution.py:408
  86.4 3.1 %copy.7 = bf16[1,128,8192]{2,1,0:T(8,128)(2,1)} copy(bf16[1,128,8192]{2,1,0:T(8,128)(2,1)} %shard_map.55) | data formatting | bytes 4194304

commit v3 on v2

--- a/solution.py
+++ b/solution.py
@@ -26,7 +26,7 @@
 def kernel(
     mask_ref, live_ref, q_hbm, k_hbm, v_hbm, out_hbm,
     kbuf, vbuf, kshift, vshift, qbuf, obuf, sbuf0, sbuf1, bias, reach, keep, mbuf, mcbuf, qs0, qs1, acc,
-    r1, r2, r3, rq, rkv, rre, ro, s1, s2, s3, sq, sq3, skv, sre, so, so3, so4,
+    r1, r2, r3, rq, rkv, rre, ro, s1, s2, s3, sq, sq3, sq4, skv, sre, sre2, so, so3, so4,
 ):
     z = lax.axis_index("section")
     s = lax.axis_index("seq")
@@ -34,7 +34,6 @@
     chip = s // 2
     x = lax.rem(chip, 4)
     y = chip // 4
-    last_row = y // 3
 
     def at(xx, yy, kk):
         return {"seq": (lax.rem(yy, 4) * 4 + lax.rem(xx, 4)) * 2 + kk}
@@ -59,13 +58,33 @@
     for d in (1, 3):
         for kk in (0, 1):
             partners.append(across(d, kk))
-            partners.append({"section": lax.rem(z + d, 4), **at(x, y + d, kk)})
     for dev in partners:
         pl.semaphore_signal(barrier, inc=1, device_id=dev, device_id_type=pl.DeviceIdType.MESH)
     pl.semaphore_wait(barrier, len(partners))
 
     pairs = ((k_hbm, kbuf), (v_hbm, vbuf))
     shifts = (kshift, vshift)
+
+    def row_in(rows):
+        hit = y == rows[0]
+        for r in rows[1:]:
+            hit = hit | (y == r)
+        return hit
+
+    def plan(p):
+        if p < 3:
+            return dict(
+                direct={1: (0, 1, 2), 2: (0, 1), 3: (0,)}, rows=(1, 2, 3, 4),
+                whole=((0, 1, 2), (0,)), half=((), (1,)), on=((1, 2), (0, 3)),
+            )
+        return dict(
+            direct={1: (0, 1, 3), 2: (0, 2), 3: (1,)}, rows=(4, 2, 3, 0),
+            whole=((0, 1, 3), (1,)), half=((2,), (0, 2)), on=((1, 3), (1, 3)),
+        )
+
+    def split(count):
+        up = min(count - 1, 1)
+        return ((0, up), (up, count - up))
 
     def stage1(p):
         for n, (src_hbm, buf) in enumerate(pairs):
@@ -80,10 +99,14 @@
                     pltpu.make_async_copy(src, dst, r1.at[p, n]).start()
                 @pl.when(core != g)
                 def _():
-                    remote(src, dst, s1.at[n, 0], r1.at[p, n], other).start()
+                    remote(src, dst, s1.at[p // 3, n, 0], r1.at[p, n], other).start()
                 for d in (1, 3, 2):
-                    dev = at(x + d, y, 0) if g == 0 else at(x, y + d, 1)
-                    remote(src, dst, s1.at[n, 3 * g + d], r1.at[p, n], dev).start()
+                    if g == 0:
+                        remote(src, dst, s1.at[p // 3, n, d], r1.at[p, n], at(x + d, y, 0)).start()
+                    else:
+                        @pl.when(row_in(plan(p)["direct"][d]))
+                        def _():
+                            remote(src, dst, s1.at[p // 3, n, 3 + d], r1.at[p, n], at(x, y + d, 1)).start()
 
     def queries(p):
         dst = qbuf.at[p, core]
@@ -98,15 +121,18 @@
                     skv.at[n], rkv.at[n], across(1, core),
                 ).start()
 
-    def ahead(kk):
-        return {"section": lax.rem(z + 1, 4), "seq": (chip - 12 * last_row) * 2 + kk}
-
     def shift_queries():
         for g in (0, 1):
             remote(
-                q_hbm.at[0, :, pl.ds(g * 4096 + 3 * 1024, 1024)], qbuf.at[3 + last_row, core],
-                sq3, rq.at[3 + last_row], ahead(g),
+                q_hbm.at[0, :, pl.ds(g * 4096 + 3 * 1024, 1024)], qbuf.at[3, core],
+                sq3, rq.at[3], across(1, g),
             ).start()
+
+    def hand_down():
+        wait_on(qbuf.at[3], rq.at[3])
+        wait_on(reach.at[1], rre.at[0])
+        remote(qbuf.at[3], qbuf.at[4], sq4, rq.at[4], at(x, y + 1, core)).start()
+        remote(reach.at[1], reach.at[2], sre2, rre.at[1], at(x, y + 1, core)).start()
 
     def wait_on(ref, sem):
         pltpu.make_async_copy(ref, ref, sem).wait()
@@ -114,27 +140,23 @@
     lower, upper = (0, 1), (1, 3)
     is_first, is_second = core == 0, core == 1
 
-    def row_in(rows):
-        hit = y == rows[0]
-        for r in rows[1:]:
-            hit = hit | (y == r)
-        return hit
-
-    def plan(p):
-        if p < 3:
-            return dict(whole=((0, 1, 2), (0,)), half=((), (1,)), on=((1, 2), (0, 3)))
-        return dict(whole=((0, 1, 3), (1,)), half=((2,), (0, 2)), on=((1, 3), (1, 3)))
-
     def moved(rows, d):
         return tuple((r + d) % 4 for r in rows)
 
-    def second_rows(p):
-        return is_second if p < 3 else is_second & (y < 3)
+    def by_count(p, body, least=0):
+        for r, count in enumerate(plan(p)["rows"]):
+            if max(count, least):
+                @pl.when(is_second & (y == r))
+                def _():
+                    body(max(count, least))
 
     def stage2(p):
         lane = pl.ds(p * 128, 128)
         for n, (_, buf) in enumerate(pairs):
-            wait_on(buf.at[0, :, :, lane], r1.at[p, n])
+            @pl.when(is_first)
+            def _():
+                wait_on(buf.at[0, :, :, lane], r1.at[p, n])
+            by_count(p, lambda c: wait_on(buf.at[0, pl.ds(0, c), :, lane], r1.at[p, n]), 1)
         for n, (_, buf) in enumerate(pairs):
             for side, d in (lower, upper):
                 def go(src, dev):
@@ -144,9 +166,7 @@
                         @pl.when(is_first & row_in(rows))
                         def _():
                             go(buf.at[y, part, :, lane], at(x, y + d, 0))
-                @pl.when(second_rows(p))
-                def _():
-                    go(buf.at[:, x, :, lane], at(x + d, y, 1))
+                by_count(p, lambda c: go(buf.at[pl.ds(0, c), x, :, lane], at(x + d, y, 1)))
 
     def stage3(p):
         lane = pl.ds(p * 128, 128)
@@ -157,9 +177,7 @@
                         @pl.when(is_first & row_in(moved(rows, d)))
                         def _():
                             wait_on(buf.at[0, pl.ds(0, size), :, lane], r2.at[p, n, side])
-                @pl.when(second_rows(p))
-                def _():
-                    wait_on(buf.at[0, :, :, lane], r2.at[p, n, side])
+                by_count(p, lambda c: wait_on(buf.at[0, pl.ds(0, c), :, lane], r2.at[p, n, side]))
         for n, (_, buf) in enumerate(pairs):
             for side, d in (lower, upper):
                 def go(src, dev):
@@ -167,20 +185,26 @@
                 @pl.when(is_first & row_in(plan(p)["on"][side]))
                 def _():
                     go(buf.at[lax.rem(y + 4 - d, 4), pl.ds(2 * side, 2), :, lane], at(x, y + d, 0))
-                @pl.when(second_rows(p))
-                def _():
-                    go(buf.at[pl.ds(2 * side, 2), lax.rem(x + 4 - d, 4), :, lane], at(x + d, y, 1))
+                def pass_on(c):
+                    start, size = split(c)[side]
+                    if size:
+                        go(buf.at[pl.ds(start, size), lax.rem(x + 4 - d, 4), :, lane], at(x + d, y, 1))
+                by_count(p, pass_on)
 
     def arrived(p):
         for n, (_, buf) in enumerate(pairs):
             for side, d in (lower, upper):
-                @pl.when((is_first & row_in(moved(plan(p)["on"][side], d))) | second_rows(p))
+                @pl.when(is_first & row_in(moved(plan(p)["on"][side], d)))
                 def _():
                     wait_on(buf.at[0, pl.ds(0, 2), :, pl.ds(0, 128)], r3.at[p, n, side])
+                def passed(c):
+                    size = split(c)[side][1]
+                    if size:
+                        wait_on(buf.at[0, pl.ds(0, size), :, pl.ds(0, 128)], r3.at[p, n, side])
+                by_count(p, passed)
 
     stage1(0)
     queries(0)
-    stage1(1)
 
     lanes = lax.broadcasted_iota(jnp.int32, (8, BLK), 1)
     first = lax.broadcasted_iota(jnp.int32, (8, BLK), 0) == 0
@@ -192,8 +216,9 @@
 
     lax.fori_loop(16, NB, reach_of, 0)
     stage2(0)
+    stage1(1)
     shift_keys()
-    remote(reach.at[0], reach.at[1 + last_row], sre, rre.at[last_row], ahead(core)).start()
+    remote(reach.at[0], reach.at[1], sre, rre.at[0], across(1, core)).start()
     shift_queries()
 
     rows = lax.broadcasted_iota(jnp.int32, (BLK, BLK), 0)
@@ -355,6 +380,9 @@
                     stage3(1)
                     stage2(2)
                     stage2(3)
+                @pl.when((t == 0) & (y == 3))
+                def _():
+                    hand_down()
                 @pl.when(t == 1)
                 def _():
                     stage3(2)
@@ -379,26 +407,39 @@
             wait_on(obuf.at[0, 0], so4.at[i])
     wait_on(qbuf.at[pl.ds(0, 3), 0], sq)
     wait_on(qbuf.at[0], sq3)
+    @pl.when(y == 3)
+    def _():
+        wait_on(qbuf.at[0], sq4)
+        wait_on(reach.at[0], sre2)
     wait_on(reach.at[0], sre)
     for n, (_, buf) in enumerate(pairs):
         wait_on(shifts[n], skv.at[n])
-        for dest in range(7):
-            wait_on(buf.at[0, pl.ds(0, 2), :, pl.ds(0, 128)], s1.at[n, dest])
         lane = pl.ds(0, 128)
         for g, p in ((0, 0), (1, 3)):
             times = pl.ds(0, 3) if g == 0 else pl.ds(0, 1)
+            half = pl.ds(0, BLK)
+            for dest in range(7):
+                def sent():
+                    wait_on(buf.at[times, 0, half, lane], s1.at[g, n, dest])
+                if dest < 4:
+                    sent()
+                else:
+                    pl.when(row_in(plan(p)["direct"][dest - 3]))(sent)
             for side in (0, 1):
                 for rows, size in ((plan(p)["whole"][side], 4), (plan(p)["half"][side], 2)):
                     if rows:
                         @pl.when(is_first & row_in(rows))
                         def _():
                             wait_on(buf.at[times, pl.ds(0, size), :, lane], s2.at[g, n, side])
-                @pl.when(second_rows(p))
-                def _():
-                    wait_on(buf.at[times, pl.ds(0, 4), :, lane], s2.at[g, n, side])
-                @pl.when((is_first & row_in(plan(p)["on"][side])) | second_rows(p))
+                @pl.when(is_first & row_in(plan(p)["on"][side]))
                 def _():
                     wait_on(buf.at[times, pl.ds(0, 2), :, lane], s3.at[g, n, side])
+                def drained(c):
+                    wait_on(buf.at[times, pl.ds(0, c), :, lane], s2.at[g, n, side])
+                    size = split(c)[side][1]
+                    if size:
+                        wait_on(buf.at[times, pl.ds(0, size), :, lane], s3.at[g, n, side])
+                by_count(p, drained)
 
 
 def per_device(queries, keys, values, block_mask, block_live):
@@ -428,7 +469,7 @@
             pltpu.VMEM((ROWS, 256), jnp.bfloat16),
             pltpu.VMEM((ROWS, 2 * HEAD_SIZE), jnp.float32),
             dma((4, 2)), dma((4, 2, 2)), dma((4, 2, 2)), dma((5,)), dma((2,)), dma((2,)), dma,
-            dma((2, 7)), dma((2, 2, 2)), dma((2, 2, 2)), dma, dma, dma((2,)), dma, dma((2,)), dma, dma((2,)),
+            dma((2, 2, 7)), dma((2, 2, 2)), dma((2, 2, 2)), dma, dma, dma, dma((2,)), dma, dma, dma((2,)), dma, dma((2,)),
         ],
         compiler_params=pltpu.CompilerParams(
             collective_id=0, has_side_effects=True, vmem_limit_bytes=60 * 1024 * 1024

time: 90.1 us -> 88.6 us (0.983)
  Pallas kernels: 86.4 us -> 85.3 us
    pallas_call x1, Pallas kernels: 86.4 us -> 85.3 us  [per_device(): pl.pallas_call(kernel, out_shape=jax.ShapeDtypeStruct(queries.shape, quer...]
where the time goes in v3:
time: 88.6 us; the launch traced here: 88.4 us
  Pallas kernels  85.3 us (96%)
  local copies, waits for them, and re-layouts  3.1 us (3%)
    pallas_call x1, Pallas kernels, per_device(): pl.pallas_call(kernel, out_shape=jax.ShapeDtypeStruct(queries.shape, quer...  85.3 us
    unnamed x1, local copies, waits for them, and re-layouts  3.1 us

profile of v3, /device:TPU:31, one launch (start us, length us, event | category | flops | bytes accessed | tf_op | source)
XLA Modules:
  0.0 88.4 jit_solution(12679634682975120154)
XLA Ops:
  0.0 85.3 %shard_map.55 = bf16[1,128,8192]{2,1,0:T(8,128)(2,1)} custom-call(s32[1,32,32]{2,1,0:T(8,128)} %mask_ref.1, s32[1,32]{1,0:T(1,128)} %live_ref.1, bf16[1,128,8192]{2,1,0:T(8,128)(2,1)} %q_hbm.1, bf16[1,128,1024]{2,1,0:T(8,128)(2,1)} %k_hbm.1, bf16[1,128,1024]{2,1,0:T(8,128)(2,1)} %v_hbm.1), custom_call_target="tpu_custom_call" | custom-call | tf_op jit(solution)/shard_map/pallas_call | solution.py:449
  85.3 3.1 %copy.7 = bf16[1,128,8192]{2,1,0:T(8,128)(2,1)} copy(bf16[1,128,8192]{2,1,0:T(8,128)(2,1)} %shard_map.55) | data formatting | bytes 4194304

commit v4 on v3

--- a/solution.py
+++ b/solution.py
@@ -14,7 +14,7 @@
 UNITS = 8 // UNIT
 ROWS = 2 * BLK * UNIT
 CH = 1024
-STEP = 512
+STEP = 1024
 COEF = 1.4426950408889634 * HEAD_SIZE ** (-0.5)
 NEG = -1e30
 
@@ -361,6 +361,9 @@
         loop(0, plain, lambda j: score(p, 0, j, False))
         loop(plain, chunks, lambda j: score(p, 0, j, True))
         settle()
+        @pl.when(t == 1)
+        def _():
+            stage3(2)
 
         for u in range(1, UNITS):
             split_queries(t, u)
@@ -385,7 +388,6 @@
                     hand_down()
                 @pl.when(t == 1)
                 def _():
-                    stage3(2)
                     stage3(3)
 
         loop(0, chunks, lambda j: weigh(p, UNITS - 1, j))

time: 88.6 us -> 88.7 us (level)
  no operation moved by 1% of the time
where the time goes in v4:
time: 88.7 us; the launch traced here: 88.5 us
  Pallas kernels  85.4 us (96%)
  local copies, waits for them, and re-layouts  3.1 us (3%)
    pallas_call x1, Pallas kernels, per_device(): pl.pallas_call(kernel, out_shape=jax.ShapeDtypeStruct(queries.shape, quer...  85.4 us
    unnamed x1, local copies, waits for them, and re-layouts  3.1 us

profile of v4, /device:TPU:31, one launch (start us, length us, event | category | flops | bytes accessed | tf_op | source)
XLA Modules:
  0.0 88.5 jit_solution(11398969050062197256)
XLA Ops:
  0.0 85.4 %shard_map.55 = bf16[1,128,8192]{2,1,0:T(8,128)(2,1)} custom-call(s32[1,32,32]{2,1,0:T(8,128)} %mask_ref.1, s32[1,32]{1,0:T(1,128)} %live_ref.1, bf16[1,128,8192]{2,1,0:T(8,128)(2,1)} %q_hbm.1, bf16[1,128,1024]{2,1,0:T(8,128)(2,1)} %k_hbm.1, bf16[1,128,1024]{2,1,0:T(8,128)(2,1)} %v_hbm.1), custom_call_target="tpu_custom_call" | custom-call | tf_op jit(solution)/shard_map/pallas_call | solution.py:451
  85.4 3.1 %copy.7 = bf16[1,128,8192]{2,1,0:T(8,128)(2,1)} copy(bf16[1,128,8192]{2,1,0:T(8,128)(2,1)} %shard_map.55) | data formatting | bytes 4194304
